TPU v7x, 32 devices: a whole 2x2x4 slice. The times are simulated.
32 devices in a mesh: groups: 2 (over y), ctx: 4 (over z), head: 2 (over x), sub: 2 (over core).
Axes of the slice: x: 2, y: 2, z: 4, core: 2. Of those that a mesh axis runs over, the one named last changes fastest.
Arguments:
- queries: bfloat16 [3072, 8192], P(('groups', 'ctx'), ('head', 'sub')), parts along dimension 0, may hold values from -60 to 60
- key_rows: bfloat16 [3072, 1024], P(('groups', 'ctx'), 'head'), parts along dimension 0, may hold values from -6 to 6
- value_rows: bfloat16 [3072, 1024], P(('groups', 'ctx'), 'head'), parts along dimension 0, may hold values from -6 to 6
- out_weight: bfloat16 [8192, 5120], P(('head', 'sub'), 'ctx'), may hold values from -0.375 to 0.375
Outputs:
- mixed: bfloat16 [3072, 5120], P(('groups', 'ctx'), ('head', 'sub')), parts along dimension 0
There are 2 independent parts, one for each index of `groups`. A program takes and returns all parts, laid end to end along the dimension named above; an argument that names none is the same for every part. Nothing has to cross between parts.
All inputs are finite; a program needn't handle non-finite values.
Results may differ from a plain program's by a relative error of at most 0.02.
Values may be sent and summed in bfloat16 or wider, within the bound.
A program may use at most 128 MiB of HBM per device.

v0:
```python
import jax
import jax.numpy as jnp
from jax import lax
from jax.sharding import PartitionSpec as P

QH = 64
KVH = 8
HD = 128


def from_behind(block, axis, distance):
    devices = range(lax.axis_size(axis))
    route = [((i - distance) % len(devices), i) for i in devices]
    return lax.ppermute(block, axis, route)


def on_device(queries, key_rows, value_rows, out_weight):
    token_count = queries.shape[0]
    heads_here = queries.shape[1] // HD
    pairs_here = key_rows.shape[1] // HD
    group_ratio = QH // KVH
    pairs_read = max(heads_here // group_ratio, 1)
    per_pair = heads_here // pairs_read
    head_offset = lax.axis_index("sub") * heads_here // group_ratio
    keys_read = lax.dynamic_slice_in_dim(
        key_rows.reshape(token_count, pairs_here, HD), head_offset, pairs_read, 1
    )
    values_read = lax.dynamic_slice_in_dim(
        value_rows.reshape(token_count, pairs_here, HD), head_offset, pairs_read, 1
    )
    stacked = jnp.stack([keys_read, values_read])
    grouped = queries.reshape(token_count, pairs_read, per_pair, HD)
    factor = 1.0 / HD**0.5

    def absorb(running, key_block, value_block):
        old_max, old_sum, old_out = running
        scores = (
            jnp.einsum("tngd,knd->tngk", grouped, key_block, preferred_element_type=jnp.float32)
            * factor
        )
        new_max = jnp.maximum(old_max, jnp.max(scores, axis=-1))
        shrink = jnp.exp(old_max - new_max)
        expo = jnp.exp(scores - new_max[..., None])
        new_sum = old_sum * shrink + jnp.sum(expo, axis=-1)
        added = jnp.einsum(
            "tngk,knd->tngd",
            expo.astype(jnp.bfloat16),
            value_block,
            preferred_element_type=jnp.float32,
        )
        return (new_max, new_sum, old_out * shrink[..., None] + added)

    empty = (
        jnp.full((token_count, pairs_read, per_pair), -1e30, jnp.float32),
        jnp.zeros((token_count, pairs_read, per_pair), jnp.float32),
        jnp.zeros((token_count, pairs_read, per_pair, HD), jnp.float32),
    )
    cycle_size = lax.axis_size("ctx")

    def forward(blocks):
        return from_behind(blocks, "ctx", 1)

    def both_turn(turn_index, loop_state):
        ahead, behind, running = loop_state
        ahead = forward(ahead)
        behind = from_behind(behind, "ctx", -1)
        running = absorb(running, ahead[0], ahead[1])
        return (ahead, behind, absorb(running, behind[0], behind[1]))

    ahead, _, final = lax.fori_loop(
        0,
        (cycle_size - 1) // 2,
        both_turn,
        (stacked, stacked, absorb(empty, keys_read, values_read)),
    )
    ahead = forward(ahead)
    final = absorb(final, ahead[0], ahead[1])
    attended = (
        (final[2] / final[1][..., None]).astype(jnp.bfloat16).reshape(token_count, heads_here * HD)
    )
    partial_value = jnp.dot(
        attended,
        lax.all_gather(out_weight, "ctx", axis=1, tiled=True),
        preferred_element_type=jnp.float32,
    )
    summed = lax.psum_scatter(
        partial_value.astype(jnp.bfloat16), ("head", "sub"), scatter_dimension=1, tiled=True
    )
    return summed


def solution(mesh):
    return jax.shard_map(
        on_device,
        mesh=mesh,
        in_specs=(
            P(("groups", "ctx"), ("head", "sub")),
            P(("groups", "ctx"), "head"),
            P(("groups", "ctx"), "head"),
            P(("head", "sub"), "ctx"),
        ),
        out_specs=P(("groups", "ctx"), ("head", "sub")),
        check_vma=False,
    )
```

profile of v0, /device:TPU:0, one launch (start us, length us, event | category | flops | bytes accessed | tf_op | source)
XLA Modules:
  0.0 442.7 jit_solution(13286977916574830429)
XLA Ops:
  6.5 0.0 all-gather.2.cloned.1.call-start
  6.5 0.7 all-gather.2.cloned.1.call-update
  7.3 0.0 reduce-scatter.2.cloned.1.call-start
  7.3 1.2 copy.17
  8.5 1.2 copy.20
  9.8 0.2 copy.50
  10.0 0.2 copy.22
  10.2 3.1 collective-permute-start
  13.3 2.1 collective-permute-start.1
  15.4 0.0 copy-done
  15.4 0.4 copy.51
  15.8 1.5 bitcast_reduce_fusion.3
  17.4 8.0 %collective-permute-done = bf16[2,384,2,128]{3,1,2,0:T(8,128)(2,1)S(1)} collective-permute-done((bf16[2,384,2,128]{3,1,2,0:T(8,128)(2,1)S(1)}, bf16[2,384,2,128]{3,1,2,0:T(8,128)(2,1)S(1)}, u32[]{:S(2)}, u32[]{:S(2)}) %collective-permute-start) | collective-permute-done | bytes 393248 | tf_op jit(solution)/shard_map/while/body/eval_jaxpr/ppermute | solution.py:14
  25.3 0.0 collective-permute-start.2
  25.4 1.5 bitcast_reduce_fusion.2
  26.8 12.9 %collective-permute-done.1 = bf16[2,384,2,128]{3,1,2,0:T(8,128)(2,1)S(1)} collective-permute-done((bf16[2,384,2,128]{3,1,2,0:T(8,128)(2,1)S(1)}, bf16[2,384,2,128]{3,1,2,0:T(8,128)(2,1)S(1)}, u32[]{:S(2)}, u32[]{:S(2)}) %collective-permute-start.1) | collective-permute-done | bytes 393248 | tf_op jit(solution)/shard_map/while/body/eval_jaxpr/ppermute | solution.py:14
  39.7 5.1 %bitcast_reduce_fusion.1 = (f32[384,2,8]{0,2,1:T(8,128)S(1)}, f32[2,384,384,8]{2,1,3,0:T(8,128)}) fusion(bf16[384,2,8,128]{3,2,1,0:T(8,128)(2,1)S(1)} %bitcast.138, bf16[2,384,2,128]{3,1,2,0:T(8,128)(2,1)S(1)} %collective-permute-done.1), kind=kOutput, calls=%fused_computation.4 | convolution fusion | flops 608692224 | bytes 11231232 | tf_op jit(solution)/shard_map/while/body/eval_jaxpr/tngd,knd->tngk/dot_general | solution.py:38
  44.8 0.0 copy-done.1
  44.8 7.7 %collective-permute-done.2 = bf16[2,384,2,128]{3,1,2,0:T(8,128)(2,1)S(1)} collective-permute-done((bf16[2,384,2,128]{3,1,2,0:T(8,128)(2,1)S(1)}, bf16[2,384,2,128]{3,1,2,0:T(8,128)(2,1)S(1)}, u32[]{:S(2)}, u32[]{:S(2)}) %collective-permute-start.2) | collective-permute-done | bytes 393248 | tf_op jit(solution)/shard_map/ppermute | solution.py:14
  52.5 5.1 %bitcast_reduce_fusion = (f32[384,2,8]{0,2,1:T(8,128)S(1)}, f32[2,384,384,8]{2,1,3,0:T(8,128)}) fusion(bf16[384,2,8,128]{3,2,1,0:T(8,128)(2,1)S(1)} %bitcast.139, bf16[2,384,2,128]{3,1,2,0:T(8,128)(2,1)S(1)} %collective-permute-done.2), kind=kOutput, calls=%fused_computation.1 | convolution fusion | flops 608692224 | bytes 11231232 | tf_op jit(solution)/shard_map/tngd,knd->tngk/dot_general | solution.py:38
  57.6 0.0 copy-done.3
  57.6 1.6 fusion.4
  59.2 0.0 copy-done.5
  59.2 1.6 fusion.6
  60.8 5.3 %fusion.8 = f32[384,2,8]{0,2,1:T(8,128)S(1)} fusion(f32[2,384,384,8]{2,1,3,0:T(8,128)} %get-tuple-element.38, f32[384,2,8]{0,2,1:T(8,128)S(1)} %get-tuple-element.30), kind=kLoop, calls=%fused_computation.16 | loop fusion | flops 7071744 | bytes 9486336 | tf_op jit(solution)/shard_map/while/body/eval_jaxpr/reduce_sum | solution.py:44
  66.1 5.2 %fusion.10 = f32[384,2,8]{0,2,1:T(8,128)S(1)} fusion(f32[2,384,384,8]{2,1,3,0:T(8,128)} %get-tuple-element.36, f32[384,2,8]{0,2,1:T(8,128)S(1)} %get-tuple-element.28), kind=kLoop, calls=%fused_computation.18 | loop fusion | flops 7071744 | bytes 9486336 | tf_op jit(solution)/shard_map/reduce_sum | solution.py:44
  71.4 0.0 copy-start.2
  71.4 0.7 multiply_add_fusion
  72.0 2.0 fusion.18
  74.1 0.0 copy-done.2
  74.1 0.0 slice-start.2
  74.1 0.0 copy-start.4
  74.1 0.0 slice-start.3
  74.1 0.0 slice-start.4
  74.2 1.8 fusion.16
  75.9 0.1 slice-done.2
  76.0 0.1 copy-done.4
  76.1 0.0 copy-start.9
  76.1 0.0 copy-start.10
  76.1 1.7 fusion.14
  77.9 1.1 slice-done.5
  78.9 0.0 copy-done.6
  79.0 0.0 copy-done.10
  79.0 3.6 fusion.29
  82.6 296.6 %all-gather.2.cloned.1.call-done = bf16[2048,5120]{1,0:T(8,128)(2,1)} async-done(((bf16[2048,1280]{1,0:T(8,128)(2,1)}), bf16[2048,5120]{1,0:T(8,128)(2,1)}) %all-gather.2.cloned.1.call-update) | async-done | bytes 20971536 | tf_op jit(solution)/shard_map/all_gather | solution.py:83
  379.1 14.5 %convolution_convert_fusion = bf16[384,5120]{1,0:T(8,128)(2,1)} fusion(bf16[384,2048]{0,1:T(8,128)(2,1)} %bitcast.147, bf16[2048,5120]{1,0:T(8,128)(2,1)} %all-gather.2.cloned.1.call-done), kind=kOutput, calls=%fused_computation.20 | convolution fusion | flops 8055029760 | bytes 26476544 | tf_op jit(solution)/shard_map/dot_general | solution.py:81
  393.7 0.0 reduce-scatter.2.cloned.1.call-update
  393.7 42.2 %reduce-scatter.2.cloned.1.call-done = bf16[384,1280]{1,0:T(8,128)(2,1)} async-done(((bf16[384,5120]{1,0:T(8,128)(2,1)}), bf16[384,1280]{1,0:T(8,128)(2,1)}) %reduce-scatter.2.cloned.1.call-update) | async-done | bytes 983056 | tf_op jit(solution)/shard_map/reduce_scatter | solution.py:86
  (22 shorter events, 0.1 us)
Async XLA Ops:
  6.5 8.9 %copy-start = (bf16[384,2048]{1,0:T(8,128)(2,1)S(1)}, bf16[384,2048]{1,0:T(8,128)(2,1)}, u32[]{:S(2)}) copy-start(bf16[384,2048]{1,0:T(8,128)(2,1)} %param.4) | copy-start | bytes 4718596
  6.5 372.6 %all-gather.2.cloned.1.call-start = ((), (), s32[]{:S(2)}) async-start(), calls=%async_computation.1 | async-start | bytes 26214400 | tf_op jit(solution)/shard_map/all_gather | solution.py:83
  7.3 428.7 %reduce-scatter.2.cloned.1.call-start = ((), (), s32[]{:S(2)}) async-start(), calls=%async_computation.2 | async-start | bytes 4915200 | tf_op jit(solution)/shard_map/reduce_scatter | solution.py:86
  10.2 15.1 %collective-permute-start = (bf16[2,384,2,128]{3,1,2,0:T(8,128)(2,1)S(1)}, bf16[2,384,2,128]{3,1,2,0:T(8,128)(2,1)S(1)}, u32[]{:S(2)}, u32[]{:S(2)}) collective-permute-start(bf16[2,384,2,128]{3,1,2,0:T(8,128)(2,1)S(1)} %pad_maximum_fusion), channel_id=1, source_target_pairs={{12,0},{0,4},{4,8},{8,12},{13,1},{1,5},{5,9},{9,13},{14,2},{2,6},{... | collective-permute-start | bytes 1179656 | tf_op jit(solution)/shard_map/while/body/eval_jaxpr/ppermute | solution.py:14
  13.3 26.4 %collective-permute-start.1 = (bf16[2,384,2,128]{3,1,2,0:T(8,128)(2,1)S(1)}, bf16[2,384,2,128]{3,1,2,0:T(8,128)(2,1)S(1)}, u32[]{:S(2)}, u32[]{:S(2)}) collective-permute-start(bf16[2,384,2,128]{3,1,2,0:T(8,128)(2,1)S(1)} %pad_maximum_fusion), channel_id=1, source_target_pairs={{4,0},{8,4},{12,8},{0,12},{5,1},{9,5},{13,9},{1,13},{6,2},{10,6},{... | collective-permute-start | bytes 1179656 | tf_op jit(solution)/shard_map/while/body/eval_jaxpr/ppermute | solution.py:14
  25.3 19.5 %copy-start.1 = (bf16[2,384,2,128]{3,1,2,0:T(8,128)(2,1)}, bf16[2,384,2,128]{3,1,2,0:T(8,128)(2,1)S(1)}, u32[]{:S(2)}) copy-start(bf16[2,384,2,128]{3,1,2,0:T(8,128)(2,1)S(1)} %collective-permute-done) | copy-start | bytes 1179652
  25.3 27.2 %collective-permute-start.2 = (bf16[2,384,2,128]{3,1,2,0:T(8,128)(2,1)S(1)}, bf16[2,384,2,128]{3,1,2,0:T(8,128)(2,1)S(1)}, u32[]{:S(2)}, u32[]{:S(2)}) collective-permute-start(bf16[2,384,2,128]{3,1,2,0:T(8,128)(2,1)S(1)} %collective-permute-done), channel_id=1, source_target_pairs={{12,0},{0,4},{4,8},{8,12},{13,1},{1,5},{5,9},{9,13},{14,2},{2,6},{... | collective-permute-start | bytes 1179656 | tf_op jit(solution)/shard_map/ppermute | solution.py:14
  39.7 17.9 %copy-start.3 = (bf16[2,384,2,128]{3,1,2,0:T(8,128)(2,1)}, bf16[2,384,2,128]{3,1,2,0:T(8,128)(2,1)S(1)}, u32[]{:S(2)}) copy-start(bf16[2,384,2,128]{3,1,2,0:T(8,128)(2,1)S(1)} %collective-permute-done.1) | copy-start | bytes 1179652
  52.5 6.7 %copy-start.5 = (bf16[2,384,2,128]{3,1,2,0:T(8,128)(2,1)}, bf16[2,384,2,128]{3,1,2,0:T(8,128)(2,1)S(1)}, u32[]{:S(2)}) copy-start(bf16[2,384,2,128]{3,1,2,0:T(8,128)(2,1)S(1)} %collective-permute-done.2) | copy-start | bytes 1179652
  71.4 2.7 copy-start.2
  72.0 3.9 slice-start
  72.0 3.9 slice-start.1
  74.1 1.9 slice-start.2
  74.1 2.0 copy-start.4
  74.1 3.7 slice-start.3
  74.1 3.7 slice-start.4
  76.1 2.9 slice-start.5
  76.1 2.9 copy-start.6
  76.1 2.9 copy-start.7
  76.1 2.9 copy-start.8
  76.1 2.9 copy-start.9
  76.1 2.9 copy-start.10
Sparse Core Ops, SparseCore 0:
  8.9 370.1 all-gather.1
  393.8 42.0 reduce-scatter.1
where the time goes:
time: 443 us
  waiting for transfers between devices  368 us (83%)
  matrix products  36.8 us (8%)
  other arithmetic  14.5 us (3%)
  between operations  13.7 us (3%)
  starting transfers between devices  5.24 us (1%)
  local copies, waits for them, and re-layouts  4.47 us (1%)
    all_gather x1, waiting for transfers between devices, on_device(): lax.all_gather(out_weight, 'ctx', axis=1, tiled=True)  297 us
    reduce_scatter x1, waiting for transfers between devices, on_device(): lax.psum_scatter(partial_value.astype(jnp.bfloat16), ('head', 'sub'), sca...  42.2 us
    ppermute x3, waiting for transfers between devices, from_behind(): return lax.ppermute(block, axis, route)  28.6 us
    dot_general x1, matrix products, on_device(): jnp.dot(attended, lax.all_gather(out_weight, 'ctx', axis=1, tiled=True),...  14.5 us
    reduce_sum x4, other arithmetic, absorb(): new_sum = old_sum * shrink + jnp.sum(expo, axis=-1)  13.7 us
    dot_general x4, matrix products, absorb(): jnp.einsum('tngd,knd->tngk', grouped, key_block, preferred_element_type=j...  13.2 us
    dot_general x4, matrix products, absorb(): jnp.einsum('tngk,knd->tngd', expo.astype(jnp.bfloat16), value_block, pref...  9.13 us
  transfers between devices with their start and end apart: 5, of which 5 were waited for; matrix products, arithmetic and copies ran while one was open for 9% of the time, Pallas kernels for 0%

commit v1 on v0

--- a/solution.py
+++ b/solution.py
@@ -6,6 +6,28 @@
 QH = 64
 KVH = 8
 HD = 128
+
+
+def joined_along(tiles, dim):
+    tiles = jnp.moveaxis(tiles, 0, dim)
+    lengths = tiles.shape
+    return tiles.reshape(*lengths[:dim], lengths[dim] * lengths[dim + 1], *lengths[dim + 2 :])
+
+
+def ring_gather(array, axis, dim):
+    length = lax.axis_size(axis)
+    pairs = [(i, (i + 1) % length) for i in range(length)]
+    back = [(b, a) for a, b in pairs]
+    lower, upper = ([], [])
+    for step in range(length - 1):
+        if step % 2 == 0:
+            lower.append(lax.ppermute(lower[-1] if lower else array, axis, pairs))
+        else:
+            upper.append(lax.ppermute(upper[-1] if upper else array, axis, back))
+    parts = jnp.stack([*lower[::-1], array, *upper])
+    shift = lax.axis_index(axis) - len(lower)
+    parts = parts[(jnp.arange(length) - shift) % length]
+    return joined_along(parts, dim)
 
 
 def from_behind(block, axis, distance):
@@ -79,9 +101,7 @@
         (final[2] / final[1][..., None]).astype(jnp.bfloat16).reshape(token_count, heads_here * HD)
     )
     partial_value = jnp.dot(
-        attended,
-        lax.all_gather(out_weight, "ctx", axis=1, tiled=True),
-        preferred_element_type=jnp.float32,
+        attended, ring_gather(out_weight, "ctx", 1), preferred_element_type=jnp.float32
     )
     summed = lax.psum_scatter(
         partial_value.astype(jnp.bfloat16), ("head", "sub"), scatter_dimension=1, tiled=True

time: 443 us -> 531 us (1.20)
  local copies, waits for them, and re-layouts: 4.47 us -> 58.8 us
  other arithmetic: 14.5 us -> 43.5 us
  waiting for transfers between devices: 368 us -> 356 us
  matrix products: 36.8 us -> 48.1 us
    all_gather x1 -> x0, waiting for transfers between devices: 297 us -> none  [on_device(): lax.all_gather(out_weight, 'ctx', axis=1, tiled=True)]
    ppermute x3, waiting for transfers between devices: 28.6 us -> 234 us  [from_behind(): return lax.ppermute(block, axis, route)]
    ppermute x0 -> x3, waiting for transfers between devices: none -> 79.9 us  [the longest x2 79.9 us: ring_gather(): lower.append(lax.ppermute(lower[-1] if lower else array, axis, pairs))]
    transpose x0 -> x1, local copies, waits for them, and re-layouts: none -> 27.3 us  [joined_along(): tiles = jnp.moveaxis(tiles, 0, dim)]
    gather x0 -> x4, local copies, waits for them, and re-layouts: none -> 26.9 us  [ring_gather(): parts = parts[(jnp.arange(length) - shift) % length]]
    transpose x0 -> x1, other arithmetic: none -> 17.3 us  [joined_along(): tiles = jnp.moveaxis(tiles, 0, dim)]
    dot_general x4, matrix products: 9.13 us -> 21 us  [absorb(): jnp.einsum('tngk,knd->tngd', expo.astype(jnp.bfloat16), value_block, pref...]
    another operation x0 -> x1, other arithmetic: none -> 8.02 us  [ring_gather(): parts = jnp.stack([*lower[::-1], array, *upper])]
  transfers between devices with their start and end apart: 5 -> 7, of which waited for: 5 -> 4; matrix products, arithmetic and copies ran while one was open for 9% -> 10% of each run, Pallas kernels for 0% -> 0%
where the time goes in v1:
time: 531 us; the launch traced here: 529 us
  waiting for transfers between devices  356 us (67%)
  local copies, waits for them, and re-layouts  58.8 us (11%)
  matrix products  48.1 us (9%)
  other arithmetic  43.5 us (8%)
  between operations  13.6 us (3%)
  starting transfers between devices  9.2 us (2%)
    ppermute x3, waiting for transfers between devices, from_behind(): return lax.ppermute(block, axis, route)  234 us
    ppermute x2, waiting for transfers between devices, ring_gather(): lower.append(lax.ppermute(lower[-1] if lower else array, axis, pairs))  79.9 us
    reduce_scatter x1, waiting for transfers between devices, on_device(): lax.psum_scatter(partial_value.astype(jnp.bfloat16), ('head', 'sub'), sca...  41.7 us
    transpose x1, local copies, waits for them, and re-layouts, joined_along(): tiles = jnp.moveaxis(tiles, 0, dim)  27.3 us
    gather x4, local copies, waits for them, and re-layouts, ring_gather(): parts = parts[(jnp.arange(length) - shift) % length]  26.9 us
    dot_general x4, matrix products, absorb(): jnp.einsum('tngk,knd->tngd', expo.astype(jnp.bfloat16), value_block, pref...  21 us
    transpose x1, other arithmetic, joined_along(): tiles = jnp.moveaxis(tiles, 0, dim)  17.3 us
    dot_general x1, matrix products, on_device(): jnp.dot(attended, ring_gather(out_weight, 'ctx', 1), preferred_element_ty...  13.9 us
  transfers between devices with their start and end apart: 7, of which 4 were waited for; matrix products, arithmetic and copies ran while one was open for 10% of the time, Pallas kernels for 0%

profile of v1, /device:TPU:0, one launch (start us, length us, event | category | flops | bytes accessed | tf_op | source)
XLA Modules:
  0.0 529.1 jit_solution(13869403447212529623)
XLA Ops:
  6.5 0.0 reduce-scatter.2.cloned.1.call-start
  6.5 3.1 collective-permute-start.3
  9.6 1.2 copy.35
  10.8 1.2 copy.32
  12.1 0.2 copy.37
  12.3 0.2 copy.66
  12.5 2.1 collective-permute-start.1
  14.6 0.0 collective-permute-start
  14.6 3.8 collective-permute-start.5
  18.4 1.8 copy.67
  20.2 1.5 bitcast_reduce_fusion.3
  21.8 120.9 %collective-permute-done = bf16[2,384,2,128]{3,1,2,0:T(8,128)(2,1)S(1)} collective-permute-done((bf16[2,384,2,128]{3,1,2,0:T(8,128)(2,1)S(1)}, bf16[2,384,2,128]{3,1,2,0:T(8,128)(2,1)S(1)}, u32[]{:S(2)}, u32[]{:S(2)}) %collective-permute-start) | collective-permute-done | bytes 393248 | tf_op jit(solution)/shard_map/while/body/eval_jaxpr/ppermute | solution.py:36
  142.7 0.0 collective-permute-start.2
  142.7 1.5 bitcast_reduce_fusion.2
  144.1 0.0 collective-permute-done.1
  144.1 5.1 bitcast_reduce_fusion.1
  149.3 113.3 %collective-permute-done.2 = bf16[2,384,2,128]{3,1,2,0:T(8,128)(2,1)S(1)} collective-permute-done((bf16[2,384,2,128]{3,1,2,0:T(8,128)(2,1)S(1)}, bf16[2,384,2,128]{3,1,2,0:T(8,128)(2,1)S(1)}, u32[]{:S(2)}, u32[]{:S(2)}) %collective-permute-start.2) | collective-permute-done | bytes 393248 | tf_op jit(solution)/shard_map/ppermute | solution.py:36
  262.6 5.1 bitcast_reduce_fusion
  267.7 0.0 collective-permute-done.3
  267.7 0.2 collective-permute-start.4
  267.9 5.2 fusion.10
  273.2 5.3 fusion.8
  278.5 1.6 fusion.6
  280.0 1.6 fusion.4
  281.7 3.5 fusion.18
  285.2 5.4 %fusion.14 = f32[2,128,384,8]{2,1,3,0:T(8,128)S(1)} fusion(f32[2,384,384,8]{2,1,3,0:T(8,128)} %get-tuple-element.40, f32[384,2,8]{0,2,1:T(8,128)S(1)} %get-tuple-element.30, bf16[2,384,2,128]{3,1,2,0:T(8,128)(2,1)S(1)} %collective-permute-done.1), kind=kOutput, calls=%fused_computation.28 | convolution fusion | flops 611057664 | bytes 12804096 | tf_op jit(solution)/shard_map/while/body/eval_jaxpr/tngk,knd->tngd/dot_general | solution.py:67
  290.6 0.0 copy-start
  290.6 0.0 slice-start
  290.7 3.4 fusion.16
  294.0 0.0 copy-done
  294.0 0.0 slice-start.1
  294.0 8.7 %fusion.29 = bf16[384,2,8,128]{0,3,2,1:T(8,128)(2,1)} fusion(f32[2,128,384,8]{2,1,3,0:T(8,128)S(1)} %fusion.14, f32[2,128,384,8]{2,1,3,0:T(8,128)} %fusion.16, f32[2,128,384,8]{2,1,3,0:T(8,128)S(1)} %copy-done, f32[2,384,384,8]{2,1,3,0:T(8,128)} %get-tuple-element.38, f32[384,2,8]{0,2,1:T(8,128)S(1)} %get-tuple-element.28, ...), kind=kOutput, calls=%fused_computation.41 | convolution fusion | flops 618135552 | bytes 20791296 | tf_op jit(solution)/shard_map/tngk,knd->tngd/dot_general | solution.py:67
  302.7 0.0 collective-permute-done.5
  302.7 79.9 %collective-permute-done.4 = bf16[2048,1280]{1,0:T(8,128)(2,1)S(1)} collective-permute-done((bf16[2048,1280]{1,0:T(8,128)(2,1)}, bf16[2048,1280]{1,0:T(8,128)(2,1)S(1)}, u32[]{:S(2)}, u32[]{:S(2)}) %collective-permute-start.4) | collective-permute-done | bytes 5242912 | tf_op jit(solution)/shard_map/ppermute | solution.py:24
  382.7 0.0 slice-done
  382.7 0.0 slice-done.1
  382.7 4.4 pad_maximum_fusion.1
  387.1 8.0 %pad_maximum_fusion = bf16[4,2048,1280]{2,1,0:T(8,128)(2,1)S(1)} fusion(bf16[1,2048,1280]{2,1,0:T(8,128)(2,1)} %bitcast.35, bf16[1,2048,1280]{2,1,0:T(8,128)(2,1)S(1)} %bitcast.151, bf16[1,2048,1280]{2,1,0:T(8,128)(2,1)} %bitcast.33, bf16[1,2048,1280]{2,1,0:T(8,128)(2,1)S(1)} %bitcast.153), kind=kLoop, calls=%fused_computation.3 | loop fusion | flops 31457280 | bytes 41943040 | tf_op jit(solution)/shard_map/stack | solution.py:27
  395.1 5.8 %fusion.54 = (bf16[4,768,1280]{2,1,0:T(8,128)(2,1)}, bf16[4,768,1280]{2,1,0:T(8,128)(2,1)}) fusion(bf16[4,2048,1280]{2,1,0:T(8,128)(2,1)S(1)} %pad_maximum_fusion), kind=kLoop, calls=%fused_computation.86 | loop fusion | bytes 31457280 | tf_op jit(solution)/shard_map/gather | solution.py:29
  400.9 5.6 %gather_fusion.2 = bf16[4,512,1280]{2,1,0:T(8,128)(2,1)} fusion(bf16[4,512,1280]{2,1,0:T(8,128)(2,1)} %pad_maximum_fusion.1, s32[1024]{0:T(1024)S(1)} %pad_clamp_fusion), kind=kCustom, calls=%fused_computation.2 | custom fusion | bytes 10485776 | tf_op jit(solution)/shard_map/gather | solution.py:29
  406.5 7.7 %gather_fusion.1 = bf16[4,768,1280]{2,1,0:T(8,128)(2,1)} fusion(bf16[4,768,1280]{2,1,0:T(8,128)(2,1)} %get-tuple-element.34, s32[1024]{0:T(1024)S(1)} %pad_clamp_fusion), kind=kCustom, calls=%fused_computation.1 | custom fusion | bytes 15728656 | tf_op jit(solution)/shard_map/gather | solution.py:29
  414.2 7.7 %gather_fusion = bf16[4,768,1280]{2,1,0:T(8,128)(2,1)} fusion(bf16[4,768,1280]{2,1,0:T(8,128)(2,1)} %get-tuple-element.33, s32[1024]{0:T(1024)S(1)} %pad_clamp_fusion), kind=kCustom, calls=%fused_computation | custom fusion | bytes 15728656 | tf_op jit(solution)/shard_map/gather | solution.py:29
  422.0 17.3 %maximum_bitcast_fusion = bf16[2048,4,1280]{2,0,1:T(8,128)(2,1)} fusion(bf16[4,512,1280]{2,1,0:T(8,128)(2,1)} %gather_fusion.2, bf16[4,768,1280]{2,1,0:T(8,128)(2,1)} %gather_fusion.1, bf16[4,768,1280]{2,1,0:T(8,128)(2,1)} %gather_fusion), kind=kLoop, calls=%fused_computation.4 | loop fusion | flops 62914560 | bytes 41943040 | tf_op jit(solution)/shard_map/transpose | solution.py:12
  439.3 27.3 %copy.47 = bf16[2048,4,1280]{0,2,1:T(8,128)(2,1)} copy(bf16[2048,4,1280]{2,0,1:T(8,128)(2,1)} %maximum_bitcast_fusion) | data formatting | bytes 41943040 | tf_op jit(solution)/shard_map/transpose | solution.py:12
  466.6 0.0 copy-done.1
  466.6 13.9 %convolution_convert_fusion = bf16[384,5120]{1,0:T(8,128)(2,1)} fusion(bf16[384,2048]{0,1:T(8,128)(2,1)S(1)} %bitcast.159, bf16[2048,5120]{0,1:T(8,128)(2,1)} %bitcast.147), kind=kOutput, calls=%fused_computation.25 | convolution fusion | flops 8055029760 | bytes 26476544 | tf_op jit(solution)/shard_map/dot_general | solution.py:103
  480.4 0.0 reduce-scatter.2.cloned.1.call-update
  480.5 41.7 %reduce-scatter.2.cloned.1.call-done = bf16[384,1280]{1,0:T(8,128)(2,1)} async-done(((bf16[384,5120]{1,0:T(8,128)(2,1)}), bf16[384,1280]{1,0:T(8,128)(2,1)}) %reduce-scatter.2.cloned.1.call-update) | async-done | bytes 983056 | tf_op jit(solution)/shard_map/reduce_scatter | solution.py:106
  (8 shorter events, 0.2 us)
Async XLA Ops:
  6.5 515.7 %reduce-scatter.2.cloned.1.call-start = ((), (), s32[]{:S(2)}) async-start(), calls=%async_computation.1 | async-start | bytes 4915200 | tf_op jit(solution)/shard_map/reduce_scatter | solution.py:106
  6.5 261.2 %collective-permute-start.3 = (bf16[2048,1280]{1,0:T(8,128)(2,1)}, bf16[2048,1280]{1,0:T(8,128)(2,1)}, u32[]{:S(2)}, u32[]{:S(2)}) collective-permute-start(bf16[2048,1280]{1,0:T(8,128)(2,1)} %param.7), channel_id=1, source_target_pairs={{0,4},{4,8},{8,12},{12,0},{1,5},{5,9},{9,13},{13,1},{2,6},{6,10},{... | collective-permute-start | bytes 15728648 | tf_op jit(solution)/shard_map/ppermute | solution.py:24
  12.5 131.6 %collective-permute-start.1 = (bf16[2,384,2,128]{3,1,2,0:T(8,128)(2,1)S(1)}, bf16[2,384,2,128]{3,1,2,0:T(8,128)(2,1)S(1)}, u32[]{:S(2)}, u32[]{:S(2)}) collective-permute-start(bf16[2,384,2,128]{3,1,2,0:T(8,128)(2,1)S(1)} %pad_maximum_fusion.2), channel_id=1, source_target_pairs={{4,0},{8,4},{12,8},{0,12},{5,1},{9,5},{13,9},{1,13},{6,2},{10,6},{... | collective-permute-start | bytes 1179656 | tf_op jit(solution)/shard_map/while/body/eval_jaxpr/ppermute | solution.py:36
  14.6 128.1 %collective-permute-start = (bf16[2,384,2,128]{3,1,2,0:T(8,128)(2,1)S(1)}, bf16[2,384,2,128]{3,1,2,0:T(8,128)(2,1)S(1)}, u32[]{:S(2)}, u32[]{:S(2)}) collective-permute-start(bf16[2,384,2,128]{3,1,2,0:T(8,128)(2,1)S(1)} %pad_maximum_fusion.2), channel_id=1, source_target_pairs={{12,0},{0,4},{4,8},{8,12},{13,1},{1,5},{5,9},{9,13},{14,2},{2,6},{... | collective-permute-start | bytes 1179656 | tf_op jit(solution)/shard_map/while/body/eval_jaxpr/ppermute | solution.py:36
  14.6 288.1 %collective-permute-start.5 = (bf16[2048,1280]{1,0:T(8,128)(2,1)}, bf16[2048,1280]{1,0:T(8,128)(2,1)}, u32[]{:S(2)}, u32[]{:S(2)}) collective-permute-start(bf16[2048,1280]{1,0:T(8,128)(2,1)} %param.7), channel_id=1, source_target_pairs={{4,0},{8,4},{12,8},{0,12},{5,1},{9,5},{13,9},{1,13},{6,2},{10,6},{... | collective-permute-start | bytes 15728648 | tf_op jit(solution)/shard_map/ppermute | solution.py:26
  142.7 119.9 %collective-permute-start.2 = (bf16[2,384,2,128]{3,1,2,0:T(8,128)(2,1)S(1)}, bf16[2,384,2,128]{3,1,2,0:T(8,128)(2,1)S(1)}, u32[]{:S(2)}, u32[]{:S(2)}) collective-permute-start(bf16[2,384,2,128]{3,1,2,0:T(8,128)(2,1)S(1)} %collective-permute-done), channel_id=1, source_target_pairs={{12,0},{0,4},{4,8},{8,12},{13,1},{1,5},{5,9},{9,13},{14,2},{2,6},{... | collective-permute-start | bytes 1179656 | tf_op jit(solution)/shard_map/ppermute | solution.py:36
  267.7 115.0 %collective-permute-start.4 = (bf16[2048,1280]{1,0:T(8,128)(2,1)}, bf16[2048,1280]{1,0:T(8,128)(2,1)S(1)}, u32[]{:S(2)}, u32[]{:S(2)}) collective-permute-start(bf16[2048,1280]{1,0:T(8,128)(2,1)} %collective-permute-done.3), channel_id=1, source_target_pairs={{0,4},{4,8},{8,12},{12,0},{1,5},{5,9},{9,13},{13,1},{2,6},{6,10},{... | collective-permute-start | bytes 15728648 | tf_op jit(solution)/shard_map/ppermute | solution.py:24
  290.6 3.4 copy-start
  290.6 92.0 %slice-start = ((s8[5242880]{0:T(1024)(128)(4,1)}), s8[1048576]{0:T(1024)(128)(4,1)S(1)}, s32[]{:S(2)}) async-start(s8[5242880]{0:T(1024)(128)(4,1)} %bitcast.148), calls=%async_computation.2 | async-start | bytes 2097152
  294.0 88.6 %slice-start.1 = ((s8[5242880]{0:T(1024)(128)(4,1)}), s8[4194304]{0:T(1024)(128)(4,1)S(1)}, s32[]{:S(2)}) async-start(s8[5242880]{0:T(1024)(128)(4,1)} %bitcast.148), calls=%async_computation.3 | async-start | bytes 8388608
  439.3 27.3 %copy-start.1 = (bf16[384,2,8,128]{0,3,2,1:T(8,128)(2,1)S(1)}, bf16[384,2,8,128]{0,3,2,1:T(8,128)(2,1)}, u32[]{:S(2)}) copy-start(bf16[384,2,8,128]{0,3,2,1:T(8,128)(2,1)} %fusion.29) | copy-start | bytes 4718596
Sparse Core Ops, SparseCore 0:
  480.6 41.5 reduce-scatter.1
